TPU v7x, 256 devices: a whole 4x4x8 slice. The times are simulated.
256 devices in a mesh: fsdp: 16 (over x, z_lo, core), pair: 16 (over z_hi, y).
Axes of the slice: x: 4, y: 4, z: 8 (z_hi: 4, z_lo: 2; z = z_hi * 2 + z_lo), core: 2. Of those that a mesh axis runs over, the one named last changes fastest.
Arguments:
- tokens: bfloat16 [32768, 8192], P('pair', 'fsdp'), may hold values from -6 to 6
- cotangent: bfloat16 [32768, 1024], P('pair', 'fsdp'), may hold values from -6 to 6
- value_weight: bfloat16 [8192, 1024], P('fsdp'), may hold values from -0.0625 to 0.0625
- adapter_down: bfloat16 [48, 8192, 128], P(None, 'fsdp'), may hold values from -0.0625 to 0.0625
- adapter_up: bfloat16 [48, 128, 1024], P(None, None, 'fsdp'), may hold values from -0.5 to 0.5
- pair_ids: int32 [64], P('pair'), may hold values from 0 to 47
- ranks: int32 [48], replicated, may hold values from 16 to 128, as said below
Outputs:
- input_grad: bfloat16 [32768, 8192], P('pair', 'fsdp')
- down_grad: bfloat16 [48, 8192, 128], P('pair', 'fsdp')
- up_grad: bfloat16 [48, 128, 1024], P('pair', None, 'fsdp')
Inputs may be any that keep to these rules, and one draw needn't show every extreme that they name: `ranks`: each rank is 128, 64, 32 or 16; both ends occur in every draw.
All inputs are finite; a program needn't handle non-finite values.
Results may differ from a plain program's by a relative error of at most 0.022.
Values may be sent and summed in bfloat16 or wider, within the bound.
A program may use at most 128 MiB of HBM per device.

v0:
```python
import math

import jax
import jax.numpy as jnp
from jax import lax
from jax.sharding import PartitionSpec as P


def per_device(tokens, cotangent, value_weight, adapter_down, adapter_up, pair_ids, ranks):
    rows, partial_gradient = tokens.shape
    kvpart = cotangent.shape[1]
    block_count = pair_ids.shape[0]
    block_length = rows // block_count
    npair, _, rmax = adapter_down.shape
    norm = 1.0 / math.sqrt(rows * lax.axis_size("pair"))
    columns = jnp.arange(rmax, dtype=jnp.int32)
    mask = (columns[None, :] < ranks[:, None]).astype(jnp.float32)
    scale = 32.0 / ranks.astype(jnp.float32)
    x_blocks = tokens.reshape(block_count, block_length, partial_gradient)
    c_blocks = cotangent.reshape(block_count, block_length, kvpart)
    selected_down_adapter = adapter_down[pair_ids]
    b_sel = adapter_up[pair_ids]
    low_part = jnp.einsum(
        "btd,bdr->btr", x_blocks, selected_down_adapter, preferred_element_type=jnp.float32
    )
    back_part = jnp.einsum("btk,brk->btr", c_blocks, b_sel, preferred_element_type=jnp.float32)
    low_full, back_full = (
        lax.psum(low_part.astype(jnp.bfloat16), "fsdp").astype(jnp.float32),
        lax.psum(back_part.astype(jnp.bfloat16), "fsdp").astype(jnp.float32),
    )
    rows_mask = mask[pair_ids][:, None, :]
    low_b = (low_full * rows_mask).astype(jnp.bfloat16)
    backward_up_part = (back_full * rows_mask).astype(jnp.bfloat16)
    whole_weight = lax.all_gather(value_weight, "fsdp", axis=0, tiled=True)
    cot_rows = lax.all_to_all(cotangent, "fsdp", split_axis=0, concat_axis=1, tiled=True)
    product = jnp.einsum(
        "tk,dk->td", cot_rows, whole_weight, preferred_element_type=jnp.float32
    ).astype(jnp.bfloat16)
    frozen_output = lax.all_to_all(product, "fsdp", split_axis=1, concat_axis=0, tiled=True)
    block_offset = scale[pair_ids]
    adapter_output = jnp.einsum(
        "eiz,efz->eif", backward_up_part, selected_down_adapter, preferred_element_type=jnp.float32
    )
    input_grad = (
        frozen_output.reshape(block_count, block_length, partial_gradient).astype(jnp.float32)
        + block_offset[:, None, None] * adapter_output
    ).astype(jnp.bfloat16)
    coef = block_offset * norm
    term_a = (
        jnp.einsum("btd,btr->bdr", x_blocks, backward_up_part, preferred_element_type=jnp.float32)
        * coef[:, None, None]
    )
    term_b = (
        jnp.einsum("btr,btk->brk", low_b, c_blocks, preferred_element_type=jnp.float32)
        * coef[:, None, None]
    )
    onehot = (pair_ids[:, None] == jnp.arange(npair, dtype=jnp.int32)[None, :]).astype(jnp.float32)
    part_a = jnp.einsum("bp,bdr->pdr", onehot, term_a)
    part_b = jnp.einsum("bp,brk->prk", onehot, term_b)
    down_grad, up_grad = (
        lax.psum_scatter(
            part_a.astype(jnp.bfloat16), "pair", scatter_dimension=0, tiled=True
        ).astype(jnp.float32),
        lax.psum_scatter(
            part_b.astype(jnp.bfloat16), "pair", scatter_dimension=0, tiled=True
        ).astype(jnp.float32),
    )
    return (
        input_grad.reshape(rows, partial_gradient),
        down_grad.astype(jnp.bfloat16),
        up_grad.astype(jnp.bfloat16),
    )


def solution(mesh):
    placed = (
        P("pair", "fsdp"),
        P("pair", "fsdp"),
        P("fsdp", None),
        P(None, "fsdp", None),
        P(None, None, "fsdp"),
        P("pair"),
        P(),
    )
    return jax.shard_map(
        per_device,
        mesh=mesh,
        in_specs=placed,
        out_specs=(P("pair", "fsdp"), P("pair", "fsdp", None), P("pair", None, "fsdp")),
        check_vma=False,
    )
```

profile of v0, /device:TPU:1, one launch (start us, length us, event | category | flops | bytes accessed | tf_op | source)
XLA Modules:
  0.0 455.5 jit_solution(17975335476844694819)
XLA Ops:
  7.2 0.8 compare_select_fusion
  8.1 3.4 gather_fusion.3
  11.5 1.7 gather_fusion.1
  13.2 2.1 fusion.1
  15.3 1.6 fusion.2
  17.0 0.7 all-gather.2.cloned.1.call-update
  17.8 0.6 gather_fusion
  18.5 0.6 gather_fusion.2
  19.1 126.9 %all-reduce.3.cloned.1.call-done = (bf16[4,512,128]{1,2,0:T(8,128)(2,1)}, bf16[4,512,128]{1,2,0:T(8,128)(2,1)}) async-done(((bf16[4,512,128]{1,2,0:T(8,128)(2,1)}, bf16[4,512,128]{1,2,0:T(8,128)(2,1)}), (bf16[4,512,128]{1,2,0:T(8,128)(2,1)}, bf16[4,512,128]{1,2,0:T(8,128)(2,1)})) %all-reduce.3.cloned.1.call-update) | async-done | bytes 1048592 | tf_op jit(solution)/shard_map/psum | solution.py:29
  145.9 1.4 convolution_multiply_fusion.1
  147.9 1.1 copy.41
  149.1 1.5 fusion
  150.6 1.1 copy.35
  151.7 3.0 convolution_convert_fusion.1
  154.7 4.3 copy.36
  159.0 16.1 %all_to_all.32 = bf16[16,128,64]{1,2,0:T(8,128)(2,1)S(1)} all-to-all(bf16[16,128,64]{1,2,0:T(8,128)(2,1)S(1)} %copy_bitcast_fusion.1), channel_id=1, replica_groups=mesh['fsdp'=16,'pair'=16] {'fsdp'}, dimensions={0} | all-to-all | bytes 524288 | tf_op jit(solution)/shard_map/all_to_all | solution.py:35
  175.2 70.6 %all-gather.2.cloned.1.call-done = bf16[8192,1024]{1,0:T(8,128)(2,1)} async-done(((bf16[512,1024]{1,0:T(8,128)(2,1)}), bf16[8192,1024]{1,0:T(8,128)(2,1)}) %all-gather.2.cloned.1.call-update) | async-done | bytes 16777232 | tf_op jit(solution)/shard_map/all_gather | solution.py:34
  245.8 12.8 %convolution_convert_fusion = bf16[128,8192]{1,0:T(8,128)(2,1)} fusion(bf16[128,1024]{0,1:T(8,128)(2,1)S(1)} %bitcast.47, bf16[8192,1024]{1,0:T(8,128)(2,1)} %all-gather.2.cloned.1.call-done), kind=kOutput, calls=%fused_computation.4 | convolution fusion | flops 2148532224 | bytes 19136512 | tf_op jit(solution)/shard_map/tk,dk->td/dot_general | solution.py:36
  258.5 1.8 copy.60
  260.3 35.4 %all_to_all.33 = bf16[128,16,512]{2,0,1:T(8,128)(2,1)S(1)} all-to-all(bf16[128,16,512]{2,0,1:T(8,128)(2,1)S(1)} %bitcast.44), channel_id=1, replica_groups=mesh['fsdp'=16,'pair'=16] {'fsdp'}, dimensions={1} | all-to-all | bytes 4194304 | tf_op jit(solution)/shard_map/all_to_all | solution.py:39
  295.8 0.6 convert_element_type.74
  296.8 2.4 add_convert_fusion
  299.2 36.5 %reduce-scatter.5.cloned.1.call-done = bf16[3,128,64]{1,2,0:T(8,128)(2,1)} async-done(((bf16[48,128,64]{1,2,0:T(8,128)(2,1)}), bf16[3,128,64]{1,2,0:T(8,128)(2,1)}) %reduce-scatter.5.cloned.1.call-update) | async-done | bytes 49168 | tf_op jit(solution)/shard_map/reduce_scatter | solution.py:64
  335.7 113.2 %reduce-scatter.3.cloned.1.call-done = bf16[3,512,128]{2,1,0:T(8,128)(2,1)} async-done(((bf16[48,512,128]{2,1,0:T(8,128)(2,1)}), bf16[3,512,128]{2,1,0:T(8,128)(2,1)}) %reduce-scatter.3.cloned.1.call-update) | async-done | bytes 393232 | tf_op jit(solution)/shard_map/reduce_scatter | solution.py:61
  (23 shorter events, 1.4 us)
Async XLA Ops:
  7.2 8.1 %copy-start = (bf16[2048,512]{1,0:T(8,128)(2,1)S(1)}, bf16[2048,512]{1,0:T(8,128)(2,1)}, u32[]{:S(2)}) copy-start(bf16[2048,512]{1,0:T(8,128)(2,1)} %param.7) | copy-start | bytes 6291460
  7.2 138.8 %copy-start.2 = (bf16[2048,64]{0,1:T(8,128)(2,1)S(1)}, bf16[2048,64]{0,1:T(8,128)(2,1)}, u32[]{:S(2)}) copy-start(bf16[2048,64]{0,1:T(8,128)(2,1)} %param.8) | copy-start | bytes 786436
  7.2 10.6 %copy-start.4 = (s32[48]{0:T(128)S(1)}, s32[48]{0:T(128)}, u32[]{:S(2)}) copy-start(s32[48]{0:T(128)} %param.13) | copy-start | bytes 580
  7.2 138.7 %all-reduce.3.cloned.1.call-start = ((), (), s32[]{:S(2)}) async-start(), calls=%async_computation.7 | async-start | bytes 2097152 | tf_op jit(solution)/shard_map/psum | solution.py:29
  11.5 135.9 %copy-start.3 = (s32[4]{0:T(128)S(1)}, s32[4]{0:T(128)}, u32[]{:S(2)}) copy-start(s32[4]{0:T(128)} %param.12) | copy-start | bytes 52
  16.9 228.8 %all-gather.2.cloned.1.call-start = ((), (), s32[]{:S(2)}) async-start(), calls=%async_computation.4 | async-start | bytes 17825792 | tf_op jit(solution)/shard_map/all_gather | solution.py:34
  17.7 318.0 %reduce-scatter.5.cloned.1.call-start = ((), (), s32[]{:S(2)}) async-start(), calls=%async_computation.6 | async-start | bytes 835584 | tf_op jit(solution)/shard_map/reduce_scatter | solution.py:64
  149.0 299.9 %reduce-scatter.3.cloned.1.call-start = ((), (), s32[]{:S(2)}) async-start(), calls=%async_computation.5 | async-start | bytes 6684672 | tf_op jit(solution)/shard_map/reduce_scatter | solution.py:61
  295.8 1.0 copy-start.1
Sparse Core Ops, SparseCore 0:
  17.1 128.8 all-reduce.2
  147.8 97.9 all-gather.1
  249.8 85.8 reduce-scatter.4
  339.9 109.0 reduce-scatter.2
where the time goes:
time: 456 us; the launch traced here: 455 us
  waiting for transfers between devices  348 us (76%)
  blocking collectives  51.6 us (11%)
  matrix products  25.3 us (6%)
  local copies, waits for them, and re-layouts  15.2 us (3%)
  between operations  13.9 us (3%)
    psum x1, waiting for transfers between devices, per_device(): lax.psum(back_part.astype(jnp.bfloat16), 'fsdp').astype(jnp.float32)  127 us
    reduce_scatter x1, waiting for transfers between devices, per_device(): lax.psum_scatter(part_a.astype(jnp.bfloat16), 'pair', scatter_dimension=0...  113 us
    all_gather x1, waiting for transfers between devices, per_device(): whole_weight = lax.all_gather(value_weight, 'fsdp', axis=0, tiled=True)  70.6 us
    reduce_scatter x1, waiting for transfers between devices, per_device(): lax.psum_scatter(part_b.astype(jnp.bfloat16), 'pair', scatter_dimension=0...  36.5 us
    all_to_all x1, blocking collectives, per_device(): lax.all_to_all(product, 'fsdp', split_axis=1, concat_axis=0, tiled=True)  35.4 us
    all_to_all x1, blocking collectives, per_device(): lax.all_to_all(cotangent, 'fsdp', split_axis=0, concat_axis=1, tiled=True)  16.1 us
    dot_general x1, matrix products, per_device(): jnp.einsum('tk,dk->td', cot_rows, whole_weight, preferred_element_type=jn...  12.8 us
  transfers between devices with their start and end apart: 4, of which 4 were waited for; matrix products, arithmetic and copies ran while one was open for 7% of the time, Pallas kernels for 0%

commit v1 on v0

v1 whole, which is shorter than its diff:
```python
import math

import jax
import jax.numpy as jnp
from jax import lax
from jax.experimental import pallas as pl
from jax.experimental.pallas import tpu as pltpu
from jax.sharding import PartitionSpec as P

MESH = pl.DeviceIdType.MESH
BF = jnp.bfloat16
F32 = jnp.float32

NAMES = ["A1", "B1R", "B1L", "B3O", "A2R", "A2L", "B2R", "B2L", "B3L", "B3R", "A3R", "A3L", "B3F", "C0", "CL", "CR", "CF"]
NAMES += ["IR", "IL", "IF"]
NAMES += ["X1R", "X1L", "X2Rb", "X2Lb", "X2Ra", "X2La", "Q1", "Q2", "Q3"]
CHUNKS = [(0, 128), (128, 128), (256, 128), (384, 128), (512, 64)]
for _k in range(len(CHUNKS)):
    NAMES += [n + str(_k) for n in ("YR", "YL", "YFR", "YFL", "Z1R", "Z1L", "Z2Rb", "Z2Lb", "Z2Ra", "Z2La")]
INDEX = {n: i for i, n in enumerate(NAMES)}


def dot(a, b, ca=1, cb=0):
    return lax.dot_general(a, b, (((ca,), (cb,)), ((), ())), preferred_element_type=F32)


def kernel(norm, ids, ranks, tok_h, cot_h, w_h, a_h, b_h, ig_h, dg_h, ug_h,
           G, xv, wv, av, bv, asel, low, backf, backb, YB, ZB, R1, R2, FL, FR,
           V, XR1, XR2, XFL, XFR, XS, QR, idt, Lm, igv, dgv, ugv, ss, rs, ls):
    f = lax.axis_index("fsdp")
    q = lax.axis_index("pair")
    x, z, c = f // 4, (f // 2) % 2, f % 2
    zh, y = q // 4, q % 4
    xr, xl, xo = (x + 1) % 4, (x + 3) % 4, (x + 2) % 4
    yr, yl, yo = (y + 1) % 4, (y + 3) % 4, (y + 2) % 4
    zr, zl = (zh + 1) % 4, (zh + 3) % 4

    def dev(xx, zz, cc):
        return {"fsdp": xx * 4 + zz * 2 + cc}

    def pdev(zz, yy):
        return {"pair": zz * 4 + yy}

    d_z, d_c, d_zc = dev(x, 1 - z, c), dev(x, z, 1 - c), dev(x, 1 - z, 1 - c)
    d_xr, d_xl = dev(xr, z, c), dev(xl, z, c)
    d_yr, d_yl = pdev(zh, yr), pdev(zh, yl)
    d_zr, d_zl = pdev(zr, y), pdev(zl, y)

    sent = []

    def send(name, src, dst, device):
        i = INDEX[name]
        copy = pltpu.make_async_remote_copy(src_ref=src, dst_ref=dst, send_sem=ss.at[i], recv_sem=rs.at[i],
                                            device_id=device, device_id_type=MESH)
        copy.start()
        sent.append(copy)

    def recv(name, dst, device):
        i = INDEX[name]
        pltpu.make_async_remote_copy(src_ref=dst, dst_ref=dst, send_sem=ss.at[i], recv_sem=rs.at[i],
                                     device_id=device, device_id_type=MESH).wait_recv()

    c_cot = pltpu.make_async_copy(cot_h, G.at[x, z, c, :, 0:2048], ls.at[0])
    c_b = pltpu.make_async_copy(b_h, bv, ls.at[1])
    c_x = pltpu.make_async_copy(tok_h, xv, ls.at[2])
    c_a = pltpu.make_async_copy(a_h, av, ls.at[3])
    c_w = pltpu.make_async_copy(w_h, wv, ls.at[4])
    for copy in (c_cot, c_b, c_x, c_a, c_w):
        copy.start()

    barrier = pltpu.get_barrier_semaphore()
    for device in (d_z, d_c, d_zc, d_xr, d_xl, d_yr, d_yl, d_zr, d_zl):
        pl.semaphore_signal(barrier, inc=1, device_id=device, device_id_type=MESH)

    lane = lax.broadcasted_iota(jnp.int32, (8, 256), 1)
    part = (lane >> 4) & 3
    tile = jnp.where(part == 0, ids[0], jnp.where(part == 1, ids[1], jnp.where(part == 2, ids[2], ids[3])))
    idt[y] = tile
    c_b.wait()
    for b in range(4):
        G[x, z, c, :, 2048 + 128 * b:2176 + 128 * b] = bv[ids[b]]
    c_cot.wait()
    pl.semaphore_wait(barrier, 9)

    send("A1", G.at[x, z, c, 0:32], G.at[x, z, c, 0:32], d_z)
    send("B1R", G.at[x, z, c, 32:64], G.at[x, z, c, 32:64], d_xr)
    send("B1L", G.at[x, z, c, 32:64], G.at[x, z, c, 32:64], d_xl)
    send("B3O", G.at[x, z, c, 32:64], G.at[x, z, c, 32:64], d_z)
    send("IR", idt.at[y], idt.at[y], d_yr)
    send("IL", idt.at[y], idt.at[y], d_yl)
    recv("A1", G.at[x, 1 - z, c, 0:32], d_z)
    send("A2R", G.at[x, :, c, 0:32], G.at[x, :, c, 0:32], d_xr)
    send("A2L", G.at[x, :, c, 0:32], G.at[x, :, c, 0:32], d_xl)
    recv("B1R", G.at[xl, z, c, 32:64], d_xl)
    send("B2R", G.at[xl, z, c, 32:48], G.at[xl, z, c, 32:48], d_xr)
    send("B3L", G.at[xl, z, c, 32:64], G.at[xl, z, c, 32:64], d_z)
    recv("B1L", G.at[xr, z, c, 32:64], d_xr)
    send("B2L", G.at[xr, z, c, 48:64], G.at[xr, z, c, 48:64], d_xl)
    send("B3R", G.at[xr, z, c, 32:64], G.at[xr, z, c, 32:64], d_z)
    recv("B3O", G.at[x, 1 - z, c, 32:64], d_z)
    send("C0", G.at[x, :, c], G.at[x, :, c], d_c)
    recv("IR", idt.at[yl], d_yl)
    send("IF", idt.at[yl], idt.at[yl], d_yr)

    c_a.wait()
    c_x.wait()
    for b in range(4):
        asel[b] = av[ids[b]]

    def rank_of(b):
        return ranks[ids[b]]

    def low_body(b, carry):
        value = dot(xv[pl.ds(pl.multiple_of(b * 512, 512), 512), :], asel[b])
        keep = lax.broadcasted_iota(jnp.int32, (512, 128), 1) < rank_of(b)
        low[b] = jnp.where(keep, value, 0.0).astype(BF)
        return carry

    lax.fori_loop(0, 4, low_body, 0)

    def features(g, start, count):
        start = pl.multiple_of(start, 128)
        return G[g, :, :, :, pl.ds(start, count)].reshape(256, count)

    def back_step(g, first):
        def body(b, carry):
            value = dot(features(g, 2048 + 128 * b, 128), features(g, 512 * b, 512), 0, 0)
            if first:
                backf[b] = value
            else:
                backf[b] = backf[b] + value
            return carry
        lax.fori_loop(0, 4, body, 0)

    recv("C0", G.at[x, :, 1 - c], d_c)
    back_step(x, True)
    recv("A2R", G.at[xl, :, c, 0:32], d_xl)
    send("A3R", G.at[xl, :, c, 0:16], G.at[xl, :, c, 0:16], d_xr)
    recv("A2L", G.at[xr, :, c, 0:32], d_xr)
    send("A3L", G.at[xr, :, c, 16:32], G.at[xr, :, c, 16:32], d_xl)
    recv("B2R", G.at[xo, z, c, 32:48], d_xl)
    recv("B2L", G.at[xo, z, c, 48:64], d_xr)
    send("B3F", G.at[xo, z, c, 32:64], G.at[xo, z, c, 32:64], d_z)
    recv("B3L", G.at[xl, 1 - z, c, 32:64], d_z)
    send("CL", G.at[xl, :, c], G.at[xl, :, c], d_c)
    recv("B3R", G.at[xr, 1 - z, c, 32:64], d_z)
    send("CR", G.at[xr, :, c], G.at[xr, :, c], d_c)
    recv("CL", G.at[xl, :, 1 - c], d_c)
    back_step(xl, False)
    recv("CR", G.at[xr, :, 1 - c], d_c)
    back_step(xr, False)
    recv("A3R", G.at[xo, :, c, 0:16], d_xl)
    recv("A3L", G.at[xo, :, c, 16:32], d_xr)
    recv("B3F", G.at[xo, 1 - z, c, 32:64], d_z)
    send("CF", G.at[xo, :, c], G.at[xo, :, c], d_c)

    recv("IL", idt.at[yr], d_yr)
    recv("IF", idt.at[yo], d_yl)
    row = lax.broadcasted_iota(jnp.int32, (192, 256), 0)
    col = lax.broadcasted_iota(jnp.int32, (192, 256), 1)
    slot = row >> 4
    turn = (slot >= 3).astype(jnp.int32) + (slot >= 6).astype(jnp.int32) + (slot >= 9).astype(jnp.int32)
    pair = 3 * (((zh + turn) & 3) * 4 + y) + slot - 3 * turn
    of_block = jnp.zeros((192, 256), jnp.int32)
    for s in range(4):
        of_block = jnp.where((col >> 6) == s, jnp.broadcast_to(idt[s][0:1, :], (192, 256)), of_block)
    hit = jnp.logical_and((row & 15) == (col & 15), of_block == pair)
    Lm[...] = jnp.where(hit, 1.0, 0.0).astype(BF)

    recv("CF", G.at[xo, :, 1 - c], d_c)
    back_step(xo, False)

    def scale_of(b):
        return 32.0 / jnp.broadcast_to(rank_of(b), (1, 128)).astype(F32)

    def mask_body(b, carry):
        keep = lax.broadcasted_iota(jnp.int32, (128, 512), 0) < rank_of(b)
        backb[b] = jnp.where(keep, backf[b], 0.0).astype(BF)
        return carry

    lax.fori_loop(0, 4, mask_body, 0)

    def y_send(k):
        r0, n = CHUNKS[k]
        own = YB.at[y, :, r0:r0 + n]
        send("YR" + str(k), own, own, d_yr)
        send("YL" + str(k), own, own, d_yl)

    def y_forward(k):
        r0, n = CHUNKS[k]
        h = n // 2
        recv("YR" + str(k), YB.at[yl, :, r0:r0 + n], d_yl)
        send("YFR" + str(k), YB.at[yl, :, r0:r0 + h], YB.at[yl, :, r0:r0 + h], d_yr)
        recv("YL" + str(k), YB.at[yr, :, r0:r0 + n], d_yr)
        send("YFL" + str(k), YB.at[yr, :, r0 + h:r0 + n], YB.at[yr, :, r0 + h:r0 + n], d_yl)

    def combine(k):
        r0, n = CHUNKS[k]
        h = n // 2
        recv("YFR" + str(k), YB.at[yo, :, r0:r0 + h], d_yl)
        recv("YFL" + str(k), YB.at[yo, :, r0 + h:r0 + n], d_yr)

        def body(i, carry):
            top = pl.ds(pl.multiple_of(r0 + 32 * i, 16), 16)
            bottom = pl.ds(pl.multiple_of(r0 + 32 * i + 16, 16), 16)
            stack = jnp.concatenate([YB[:, :, top, :].reshape(256, 128), YB[:, :, bottom, :].reshape(256, 128)], axis=1)
            out = dot(Lm[...], stack).astype(BF)
            ZB[:, :, top, :] = out[:, 0:128].reshape(4, 3, 16, 128)
            ZB[:, :, bottom, :] = out[:, 128:256].reshape(4, 3, 16, 128)
            return carry

        lax.fori_loop(0, n // 32, body, 0)
        s0 = r0 // 2
        send("Z1R" + str(k), ZB.at[2, :, r0:r0 + h], R1.at[:, s0:s0 + h], d_zr)
        send("Z1L" + str(k), ZB.at[2, :, r0 + h:r0 + n], R2.at[:, s0:s0 + h], d_zl)
        send("Z2Rb" + str(k), ZB.at[1, :, r0 + h:r0 + n], FL.at[:, r0 + h:r0 + n], d_zr)
        send("Z2Lb" + str(k), ZB.at[3, :, r0:r0 + h], FR.at[:, r0:r0 + h], d_zl)

    def pass_on(k):
        r0, n = CHUNKS[k]
        h = n // 2
        s0 = r0 // 2
        recv("Z1R" + str(k), R1.at[:, s0:s0 + h], d_zl)
        ZB[1, :, r0:r0 + h] = (ZB[1, :, r0:r0 + h].astype(F32) + R1[:, s0:s0 + h].astype(F32)).astype(BF)
        send("Z2Ra" + str(k), ZB.at[1, :, r0:r0 + h], FL.at[:, r0:r0 + h], d_zr)
        recv("Z1L" + str(k), R2.at[:, s0:s0 + h], d_zr)
        ZB[3, :, r0 + h:r0 + n] = (ZB[3, :, r0 + h:r0 + n].astype(F32) + R2[:, s0:s0 + h].astype(F32)).astype(BF)
        send("Z2La" + str(k), ZB.at[3, :, r0 + h:r0 + n], FR.at[:, r0 + h:r0 + n], d_zl)

    outs = []

    def finish(k):
        r0, n = CHUNKS[k]
        h = n // 2
        recv("Z2Rb" + str(k), FL.at[:, r0 + h:r0 + n], d_zl)
        recv("Z2Lb" + str(k), FR.at[:, r0:r0 + h], d_zr)
        recv("Z2Ra" + str(k), FL.at[:, r0:r0 + h], d_zl)
        recv("Z2La" + str(k), FR.at[:, r0 + h:r0 + n], d_zr)
        total = (ZB[0, :, r0:r0 + n].astype(F32) + FL[:, r0:r0 + n].astype(F32) + FR[:, r0:r0 + n].astype(F32)).astype(BF)
        if r0 < 512:
            dgv[:, r0:r0 + n] = total
            copy = pltpu.make_async_copy(dgv.at[:, r0:r0 + n], dg_h.at[:, r0:r0 + n], ls.at[9 + k])
        else:
            ugv[...] = total
            copy = pltpu.make_async_copy(ugv, ug_h, ls.at[9 + k])
        copy.start()
        outs.append(copy)

    def down_term(k):
        def body(b, carry):
            rows = pl.ds(pl.multiple_of(b * 512, 512), 512)
            value = dot(backb[b], xv[rows, 128 * k:128 * k + 128])
            YB[y, b, 128 * k:128 * k + 128, :] = (value.T * (scale_of(b) * norm)).astype(BF)
            return carry
        lax.fori_loop(0, 4, body, 0)

    def input_grad(b):
        ad = scale_of(b)[:, 0:1]

        def body(i, carry):
            rows = pl.ds(pl.multiple_of(i * 128, 128), 128)
            acc = dot(wv[rows, 0:256], features(0, 512 * b, 512))
            for g in range(1, 4):
                acc = acc + dot(wv[rows, 256 * g:256 * g + 256], features(g, 512 * b, 512))
            extra = dot(asel[b, rows, :], backb[b])
            value = acc.astype(BF).astype(F32) + ad * extra
            igv[512 * b:512 * b + 512, rows] = value.T.astype(BF)
            return carry

        lax.fori_loop(0, 4, body, 0)
        copy = pltpu.make_async_copy(igv.at[512 * b:512 * b + 512], ig_h.at[512 * b:512 * b + 512], ls.at[5 + b])
        copy.start()
        outs.append(copy)

    for k in range(4):
        down_term(k)
        y_send(k)

    def up_body(i, carry):
        g, b = i // 4, i % 4
        V[g, b] = dot(features(g, 512 * b, 512), low[b]).astype(BF)
        return carry

    lax.fori_loop(0, 16, up_body, 0)
    send("X1R", V.at[xo, :, 0:128], XR1, d_xr)
    send("X1L", V.at[xo, :, 128:256], XR2, d_xl)
    send("X2Rb", V.at[xr, :, 128:256], XFL.at[:, 128:256], d_xr)
    send("X2Lb", V.at[xl, :, 0:128], XFR.at[:, 0:128], d_xl)

    y_forward(0)
    recv("X1R", XR1, d_xl)
    V[xr, :, 0:128] = (V[xr, :, 0:128].astype(F32) + XR1[...].astype(F32)).astype(BF)
    send("X2Ra", V.at[xr, :, 0:128], XFL.at[:, 0:128], d_xr)
    recv("X1L", XR2, d_xr)
    V[xl, :, 128:256] = (V[xl, :, 128:256].astype(F32) + XR2[...].astype(F32)).astype(BF)
    send("X2La", V.at[xl, :, 128:256], XFR.at[:, 128:256], d_xl)
    combine(0)
    y_forward(1)
    pass_on(0)
    combine(1)
    recv("X2Rb", XFL.at[:, 128:256], d_xl)
    recv("X2Lb", XFR.at[:, 0:128], d_xr)
    recv("X2Ra", XFL.at[:, 0:128], d_xl)
    recv("X2La", XFR.at[:, 128:256], d_xr)
    for s in range(4):
        rows = slice(64 * s, 64 * s + 64)
        XS[s] = (V[x, :, rows].astype(F32) + XFL[:, rows].astype(F32) + XFR[:, rows].astype(F32)).astype(BF)
    me = z * 2 + c
    o1, o2, o3 = (1 - z) * 2 + c, z * 2 + 1 - c, (1 - z) * 2 + 1 - c
    send("Q1", XS.at[o1], QR.at[me], d_z)
    send("Q2", XS.at[o2], QR.at[me], d_c)
    send("Q3", XS.at[o3], QR.at[me], d_zc)
    c_w.wait()
    y_forward(2)
    pass_on(1)
    combine(2)
    recv("Q1", QR.at[o1], d_z)
    recv("Q2", QR.at[o2], d_c)
    recv("Q3", QR.at[o3], d_zc)

    def own_body(b, carry):
        total = XS[me, b].astype(F32) + QR[o1, b].astype(F32) + QR[o2, b].astype(F32) + QR[o3, b].astype(F32)
        YB[y, b, 512:576, :] = (total * (scale_of(b) * norm)).astype(BF)
        return carry

    lax.fori_loop(0, 4, own_body, 0)
    y_send(4)
    y_forward(3)
    pass_on(2)
    combine(3)
    y_forward(4)
    input_grad(0)
    pass_on(3)
    combine(4)
    input_grad(1)
    pass_on(4)
    input_grad(2)
    input_grad(3)
    for k in range(5):
        finish(k)
    for copy in outs:
        copy.wait()
    for copy in sent:
        copy.wait_send()


def per_device(tokens, cotangent, value_weight, adapter_down, adapter_up, pair_ids, ranks):
    rows, width = tokens.shape
    norm = 1.0 / math.sqrt(rows * lax.axis_size("pair"))
    cot = cotangent.T
    up = jnp.swapaxes(adapter_up, 1, 2)
    any_spec = pl.BlockSpec(memory_space=pl.ANY)
    smem = pl.BlockSpec(memory_space=pltpu.SMEM)
    count = len(NAMES)
    vm = pltpu.VMEM
    import functools
    out = pl.pallas_call(
        functools.partial(kernel, norm),
        out_shape=(
            jax.ShapeDtypeStruct((2048, 512), BF),
            jax.ShapeDtypeStruct((3, 512, 128), BF),
            jax.ShapeDtypeStruct((3, 64, 128), BF),
        ),
        in_specs=[smem, smem] + [any_spec] * 5,
        out_specs=(any_spec,) * 3,
        scratch_shapes=[
            vm((4, 2, 2, 64, 2560), BF),
            vm((2048, 512), BF),
            vm((512, 1024), BF),
            vm((48, 512, 128), BF),
            vm((48, 64, 128), BF),
            vm((4, 512, 128), BF),
            vm((4, 512, 128), BF),
            vm((4, 128, 512), F32),
            vm((4, 128, 512), BF),
            vm((4, 4, 576, 128), BF),
            vm((4, 3, 576, 128), BF),
            vm((3, 288, 128), BF),
            vm((3, 288, 128), BF),
            vm((3, 576, 128), BF),
            vm((3, 576, 128), BF),
            vm((4, 4, 256, 128), BF),
            vm((4, 128, 128), BF),
            vm((4, 128, 128), BF),
            vm((4, 256, 128), BF),
            vm((4, 256, 128), BF),
            vm((4, 4, 64, 128), BF),
            vm((4, 4, 64, 128), BF),
            vm((4, 8, 256), jnp.int32),
            vm((192, 256), BF),
            vm((2048, 512), BF),
            vm((3, 512, 128), BF),
            vm((3, 64, 128), BF),
            pltpu.SemaphoreType.DMA((count,)),
            pltpu.SemaphoreType.DMA((count,)),
            pltpu.SemaphoreType.DMA((14,)),
        ],
        compiler_params=pltpu.CompilerParams(
            collective_id=0, has_side_effects=True, vmem_limit_bytes=60 * 1024 * 1024
        ),
    )(pair_ids, ranks, tokens, cot, value_weight, adapter_down, up)
    return out[0], out[1], jnp.swapaxes(out[2], 1, 2)


def solution(mesh):
    placed = (
        P("pair", "fsdp"),
        P("pair", "fsdp"),
        P("fsdp", None),
        P(None, "fsdp", None),
        P(None, None, "fsdp"),
        P("pair"),
        P(),
    )
    return jax.shard_map(
        per_device,
        mesh=mesh,
        in_specs=placed,
        out_specs=(P("pair", "fsdp"), P("pair", "fsdp", None), P("pair", None, "fsdp")),
        check_vma=False,
    )
```

time: 456 us -> 97.2 us (0.21)
  waiting for transfers between devices: 348 us -> 0 us
  Pallas kernels: 0 us -> 92 us
  blocking collectives: 51.6 us -> 0 us
  matrix products: 25.3 us -> 0 us
  between operations: 13.9 us -> 0.66 us
  local copies, waits for them, and re-layouts: 15.2 us -> 4.47 us
    reduce_scatter x2 -> x0, waiting for transfers between devices: 150 us -> none  [the longest x1 113 us: per_device(): lax.psum_scatter(part_a.astype(jnp.bfloat16), 'pair', scatter_dimension=0...]
    psum x1 -> x0, waiting for transfers between devices: 127 us -> none  [per_device(): lax.psum(back_part.astype(jnp.bfloat16), 'fsdp').astype(jnp.float32)]
    pallas_call x0 -> x1, Pallas kernels: none -> 92 us  [per_device(): pl.pallas_call(functools.partial(kernel, norm), out_shape=(jax.ShapeDtype...]
    all_gather x1 -> x0, waiting for transfers between devices: 70.6 us -> none  [per_device(): whole_weight = lax.all_gather(value_weight, 'fsdp', axis=0, tiled=True)]
    all_to_all x2 -> x0, blocking collectives: 51.6 us -> none  [the longest x1 35.4 us: per_device(): lax.all_to_all(product, 'fsdp', split_axis=1, concat_axis=0, tiled=True)]
    dot_general x8 -> x0, matrix products: 25.3 us -> none  [the longest x1 12.8 us: per_device(): jnp.einsum('tk,dk->td', cot_rows, whole_weight, preferred_element_type=jn...]
    gather x4 -> x0, local copies, waits for them, and re-layouts: 6.33 us -> none  [the longest x1 3.43 us: per_device(): selected_down_adapter = adapter_down[pair_ids]]
    convert_element_type x2 -> x0, local copies, waits for them, and re-layouts: 5.39 us -> none  [the longest x1 4.28 us: per_device(): part_a.astype(jnp.bfloat16)]
  transfers between devices with their start and end apart: 4 -> 0, of which waited for: 4 -> 0; matrix products, arithmetic and copies ran while one was open for 7% -> 0% of each run, Pallas kernels for 0% -> 0%
where the time goes in v1:
time: 97.2 us; the launch traced here: 97.1 us
  Pallas kernels  92 us (95%)
  local copies, waits for them, and re-layouts  4.47 us (5%)
    pallas_call x1, Pallas kernels, per_device(): pl.pallas_call(functools.partial(kernel, norm), out_shape=(jax.ShapeDtype...  92 us
    unnamed x7, local copies, waits for them, and re-layouts  4.47 us

profile of v1, /device:TPU:1, one launch (start us, length us, event | category | flops | bytes accessed | tf_op | source)
XLA Modules:
  0.0 97.1 jit_solution(14025816662031069305)
XLA Ops:
  0.6 92.0 %shard_map.94 = (bf16[2048,512]{1,0:T(8,128)(2,1)}, bf16[3,512,128]{2,1,0:T(8,128)(2,1)}, bf16[3,64,128]{2,1,0:T(8,128)(2,1)}) custom-call(s32[4]{0:T(128)} %ids.1, s32[48]{0:T(128)} %ranks.1, bf16[2048,512]{1,0:T(8,128)(2,1)} %tok_h.1, bf16[64,2048]{1,0:T(8,128)(2,1)} %bitcast.4, bf16[512,1024]{1,0:T(8,128)(2,1)} %w_h.1, bf16[48,512,128]{2,1,0:T(8,128)(2,1)} %a_h.1, ...), custom_call_target="tpu_custom_call" | custom-call | tf_op jit(solution)/shard_map/pallas_call | solution.py:357
  92.6 0.0 copy-start
  92.6 0.0 copy-start.1
  92.6 3.1 %copy.13 = bf16[2048,512]{1,0:T(8,128)(2,1)} copy(bf16[2048,512]{1,0:T(8,128)(2,1)} %get-tuple-element.12) | data formatting | bytes 4194304
  95.7 0.0 copy-done
  95.7 0.7 copy.14
  96.5 0.0 copy-done.1
  96.5 0.6 copy.15
Async XLA Ops:
  92.6 3.1 %copy-start = (bf16[3,512,128]{2,1,0:T(8,128)(2,1)S(1)}, bf16[3,512,128]{2,1,0:T(8,128)(2,1)}, u32[]{:S(2)}) copy-start(bf16[3,512,128]{2,1,0:T(8,128)(2,1)} %get-tuple-element.13) | copy-start | bytes 1179652
  92.6 3.9 %copy-start.1 = (bf16[3,64,128]{2,1,0:T(8,128)(2,1)S(1)}, bf16[3,64,128]{2,1,0:T(8,128)(2,1)}, u32[]{:S(2)}) copy-start(bf16[3,64,128]{2,1,0:T(8,128)(2,1)} %get-tuple-element.8) | copy-start | bytes 147460

commit v2 on v1

v2 whole, which is shorter than its diff:
```python
import math

import jax
import jax.numpy as jnp
from jax import lax
from jax.experimental import pallas as pl
from jax.experimental.pallas import tpu as pltpu
from jax.sharding import PartitionSpec as P

MESH = pl.DeviceIdType.MESH
BF = jnp.bfloat16
F32 = jnp.float32

NAMES = ["A1", "B1R", "B1L", "B3O", "A2R", "A2L", "A2RZ", "A2LZ", "B2R", "B2L", "B3L", "B3R", "A3R", "A3L", "A3RZ", "A3LZ", "B3F", "C0", "CL", "CR", "CF"]
NAMES += ["IR", "IL", "IF", "JR", "JL", "JF"]
NAMES += ["X1R", "X1L", "X2Rb", "X2Lb", "X2Ra", "X2La", "Q1", "Q2"]
CHUNKS = [(0, 32), (32, 96), (128, 64), (192, 96), (288, 128), (416, 96), (512, 64)]
SWAPPED = 1
for _k in range(len(CHUNKS)):
    NAMES += [n + str(_k) for n in ("YR", "YL", "YFR", "YFL", "Z1R", "Z1L", "Z2Rb", "Z2Lb", "Z2Ra", "Z2La")]
INDEX = {n: i for i, n in enumerate(NAMES)}


def dot(a, b, ca=1, cb=0):
    return lax.dot_general(a, b, (((ca,), (cb,)), ((), ())), preferred_element_type=F32)


def kernel(norm, ids, ranks, tok_h, cot_h, w_h, a_h, b_h, igv, dgv, ugv,
           G, xv, wv, av, bv, asel, low, backf, backb, YB, ZB, R1, R2, FL, FR,
           V, XR1, XR2, XFL, XFR, XS, QR, idt, jdt, Lm, ss, rs, ls):
    f = lax.axis_index("fsdp")
    q = lax.axis_index("pair")
    x, z, c = f // 4, (f // 2) % 2, f % 2
    zh, y = q // 4, q % 4
    xr, xl, xo = (x + 1) % 4, (x + 3) % 4, (x + 2) % 4
    yr, yl, yo = (y + 1) % 4, (y + 3) % 4, (y + 2) % 4
    zr, zl, zo = (zh + 1) % 4, (zh + 3) % 4, (zh + 2) % 4

    def dev(xx, zz, cc):
        return {"fsdp": xx * 4 + zz * 2 + cc}

    def pdev(zz, yy):
        return {"pair": zz * 4 + yy}

    d_z, d_c = dev(x, 1 - z, c), dev(x, z, 1 - c)
    d_xr, d_xl = dev(xr, z, c), dev(xl, z, c)
    d_yr, d_yl = pdev(zh, yr), pdev(zh, yl)
    d_zr, d_zl = pdev(zr, y), pdev(zl, y)

    plain = ((y, yl, yr, yo), d_yl, d_yr, d_zl, d_zr)
    swapped = ((zh, zl, zr, zo), d_zl, d_zr, d_yl, d_yr)
    role = [swapped if k == SWAPPED else plain for k in range(len(CHUNKS))]

    sent = {}

    def send(name, src, dst, device):
        i = INDEX[name]
        copy = pltpu.make_async_remote_copy(src_ref=src, dst_ref=dst, send_sem=ss.at[i], recv_sem=rs.at[i],
                                            device_id=device, device_id_type=MESH)
        copy.start()
        sent[name] = copy

    def gone(*names):
        for name in names:
            sent.pop(name).wait_send()

    def recv(name, dst, device):
        i = INDEX[name]
        pltpu.make_async_remote_copy(src_ref=dst, dst_ref=dst, send_sem=ss.at[i], recv_sem=rs.at[i],
                                     device_id=device, device_id_type=MESH).wait_recv()

    c_cot = pltpu.make_async_copy(cot_h, G.at[x, z, c, :, 0:2048], ls.at[0])
    c_cot.start()
    c_b = pltpu.make_async_copy(b_h, bv, ls.at[1])
    c_b.start()

    barrier = pltpu.get_barrier_semaphore()
    for device in (d_z, d_c, d_xr, d_xl, d_yr, d_yl, d_zr, d_zl):
        pl.semaphore_signal(barrier, inc=1, device_id=device, device_id_type=MESH)

    lane = lax.broadcasted_iota(jnp.int32, (8, 256), 1)
    part = (lane >> 4) & 3
    tile = jnp.where(part == 0, ids[0], jnp.where(part == 1, ids[1], jnp.where(part == 2, ids[2], ids[3])))
    idt[y] = tile
    jdt[zh] = tile
    c_x = pltpu.make_async_copy(tok_h, xv, ls.at[2])
    c_a = pltpu.make_async_copy(a_h, av, ls.at[3])
    c_w = pltpu.make_async_copy(w_h, wv, ls.at[4])

    L0, L1 = slice(0, 1408), slice(1408, 2560)

    def relay(name, part, device):
        send(name, part, part, device)

    c_cot.wait()
    pl.semaphore_wait(barrier, 8)
    relay("A1", G.at[x, z, c, :, L0], d_z)
    c_b.wait()
    for b in range(4):
        G[x, z, c, :, 2048 + 128 * b:2176 + 128 * b] = bv[ids[b]]
    relay("B1R", G.at[x, z, c, :, L1], d_xr)
    relay("B1L", G.at[x, z, c, :, L1], d_xl)
    relay("B3O", G.at[x, z, c, :, L1], d_z)
    relay("A2R", G.at[x, z, c, :, L0], d_xr)
    relay("A2L", G.at[x, z, c, :, L0], d_xl)
    for copy in (c_x, c_a, c_w):
        copy.start()
    relay("IR", idt.at[y], d_yr)
    relay("IL", idt.at[y], d_yl)
    relay("JR", jdt.at[zh], d_zr)
    relay("JL", jdt.at[zh], d_zl)

    def rank_of(b):
        return ranks[ids[b]]

    def scale_of(b):
        return 32.0 / jnp.broadcast_to(rank_of(b), (1, 128)).astype(F32)

    def features(g, start, count):
        start = pl.multiple_of(start, 128)
        return G[g, :, :, :, pl.ds(start, count)].reshape(256, count)

    def low_all():
        for b in range(4):
            asel[b] = av[ids[b]]

        def body(b, carry):
            value = dot(xv[pl.ds(pl.multiple_of(b * 512, 512), 512), :], asel[b])
            keep = lax.broadcasted_iota(jnp.int32, (512, 128), 1) < rank_of(b)
            low[b] = jnp.where(keep, value, 0.0).astype(BF)
            return carry

        lax.fori_loop(0, 4, body, 0)

    def back_step(g, first):
        for b in range(4):
            value = dot(features(g, 2048 + 128 * b, 128), features(g, 512 * b, 512), 0, 0)
            if first:
                backf[b] = value
            else:
                backf[b] = backf[b] + value

    def back_last(g):
        for b in range(4):
            value = backf[b] + dot(features(g, 2048 + 128 * b, 128), features(g, 512 * b, 512), 0, 0)
            keep = lax.broadcasted_iota(jnp.int32, (128, 512), 0) < rank_of(b)
            backb[b] = jnp.where(keep, value, 0.0).astype(BF)

    def up_step(g):
        def body(b, carry):
            V[g, b] = dot(features(g, 512 * b, 512), low[b]).astype(BF)
            return carry
        lax.fori_loop(0, 4, body, 0)

    def onehot(which):
        row = lax.broadcasted_iota(jnp.int32, (192, 256), 0)
        col = lax.broadcasted_iota(jnp.int32, (192, 256), 1)
        slot = row >> 4
        turn = (slot >= 3).astype(jnp.int32) + (slot >= 6).astype(jnp.int32) + (slot >= 9).astype(jnp.int32)
        if which:
            owner = zh * 4 + ((y + turn) & 3)
        else:
            owner = ((zh + turn) & 3) * 4 + y
        pair = 3 * owner + slot - 3 * turn
        of_block = jnp.zeros((192, 256), jnp.int32)
        table = jdt if which else idt
        for s in range(4):
            of_block = jnp.where((col >> 6) == s, jnp.broadcast_to(table[s][0:1, :], (192, 256)), of_block)
        hit = jnp.logical_and((row & 15) == (col & 15), of_block == pair)
        Lm[which] = jnp.where(hit, 1.0, 0.0).astype(BF)

    def y_send(k):
        r0, n = CHUNKS[k]
        (me, _, _, _), al, ar, _, _ = role[k]
        own = YB.at[me, :, r0:r0 + n]
        relay("YR" + str(k), own, ar)
        relay("YL" + str(k), own, al)

    def y_forward(k):
        r0, n = CHUNKS[k]
        h = n // 2
        (_, il, ir, _), al, ar, _, _ = role[k]
        recv("YR" + str(k), YB.at[il, :, r0:r0 + n], al)
        relay("YFR" + str(k), YB.at[il, :, r0:r0 + h], ar)
        recv("YL" + str(k), YB.at[ir, :, r0:r0 + n], ar)
        relay("YFL" + str(k), YB.at[ir, :, r0 + h:r0 + n], al)

    def combine_math(k):
        r0, n = CHUNKS[k]
        which = 1 if k == SWAPPED else 0

        def body(i, carry):
            top = pl.ds(pl.multiple_of(r0 + 32 * i, 16), 16)
            bottom = pl.ds(pl.multiple_of(r0 + 32 * i + 16, 16), 16)
            stack = jnp.concatenate([YB[:, :, top, :].reshape(256, 128), YB[:, :, bottom, :].reshape(256, 128)], axis=1)
            out = dot(Lm[which], stack).astype(BF)
            ZB[:, :, top, :] = out[:, 0:128].reshape(4, 3, 16, 128)
            ZB[:, :, bottom, :] = out[:, 128:256].reshape(4, 3, 16, 128)
            return carry

        lax.fori_loop(0, n // 32, body, 0)

    def combine(k):
        r0, n = CHUNKS[k]
        h = n // 2
        s0 = r0 // 2
        (_, _, _, io), al, ar, bl, br = role[k]
        recv("YFR" + str(k), YB.at[io, :, r0:r0 + h], al)
        recv("YFL" + str(k), YB.at[io, :, r0 + h:r0 + n], ar)
        combine_math(k)
        send("Z1R" + str(k), ZB.at[2, :, r0:r0 + h], R1.at[:, s0:s0 + h], br)
        send("Z1L" + str(k), ZB.at[2, :, r0 + h:r0 + n], R2.at[:, s0:s0 + h], bl)

    def z_rest(k):
        r0, n = CHUNKS[k]
        h = n // 2
        _, _, _, bl, br = role[k]
        send("Z2Rb" + str(k), ZB.at[1, :, r0 + h:r0 + n], FL.at[:, r0 + h:r0 + n], br)
        send("Z2Lb" + str(k), ZB.at[3, :, r0:r0 + h], FR.at[:, r0:r0 + h], bl)

    def pass_on(k):
        r0, n = CHUNKS[k]
        h = n // 2
        s0 = r0 // 2
        _, _, _, bl, br = role[k]
        recv("Z1R" + str(k), R1.at[:, s0:s0 + h], bl)
        ZB[1, :, r0:r0 + h] = (ZB[1, :, r0:r0 + h].astype(F32) + R1[:, s0:s0 + h].astype(F32)).astype(BF)
        send("Z2Ra" + str(k), ZB.at[1, :, r0:r0 + h], FL.at[:, r0:r0 + h], br)
        recv("Z1L" + str(k), R2.at[:, s0:s0 + h], br)
        ZB[3, :, r0 + h:r0 + n] = (ZB[3, :, r0 + h:r0 + n].astype(F32) + R2[:, s0:s0 + h].astype(F32)).astype(BF)
        send("Z2La" + str(k), ZB.at[3, :, r0 + h:r0 + n], FR.at[:, r0 + h:r0 + n], bl)

    def finish(k):
        r0, n = CHUNKS[k]
        h = n // 2
        _, _, _, bl, br = role[k]
        recv("Z2Rb" + str(k), FL.at[:, r0 + h:r0 + n], bl)
        recv("Z2Lb" + str(k), FR.at[:, r0:r0 + h], br)
        recv("Z2Ra" + str(k), FL.at[:, r0:r0 + h], bl)
        recv("Z2La" + str(k), FR.at[:, r0 + h:r0 + n], br)
        total = (ZB[0, :, r0:r0 + n].astype(F32) + FL[:, r0:r0 + n].astype(F32) + FR[:, r0:r0 + n].astype(F32)).astype(BF)
        if r0 < 512:
            dgv[:, r0:r0 + n] = total
        else:
            ugv[...] = total

    def down_term(k):
        for b in range(4):
            value = dot(backb[b], xv[512 * b:512 * b + 512, 128 * k:128 * k + 128])
            value = (value.T * (scale_of(b) * norm)).astype(BF)
            if k == 0:
                YB[y, b, 0:32, :] = value[0:32]
                YB[zh, b, 32:128, :] = value[32:128]
            else:
                YB[y, b, 128 * k:128 * k + 128, :] = value

    def input_grad(b):
        ad = scale_of(b)[:, 0:1]

        def body(i, carry):
            rows = pl.ds(pl.multiple_of(i * 128, 128), 128)
            acc = dot(wv[rows, 0:256], features(0, 512 * b, 512))
            for g in range(1, 4):
                acc = acc + dot(wv[rows, 256 * g:256 * g + 256], features(g, 512 * b, 512))
            extra = dot(asel[b, rows, :], backb[b])
            value = acc.astype(BF).astype(F32) + ad * extra
            igv[512 * b:512 * b + 512, rows] = value.T.astype(BF)
            return carry

        lax.fori_loop(0, 4, body, 0)

    c_a.wait()
    c_x.wait()
    low_all()
    recv("B1R", G.at[xl, z, c, :, L1], d_xl)
    relay("B2R", G.at[xl, z, c, 0:32, L1], d_xr)
    relay("B3L", G.at[xl, z, c, :, L1], d_z)
    recv("B1L", G.at[xr, z, c, :, L1], d_xr)
    relay("B2L", G.at[xr, z, c, 32:64, L1], d_xl)
    relay("B3R", G.at[xr, z, c, :, L1], d_z)
    recv("A1", G.at[x, 1 - z, c, :, L0], d_z)
    relay("A2RZ", G.at[x, 1 - z, c, :, L0], d_xr)
    relay("A2LZ", G.at[x, 1 - z, c, :, L0], d_xl)
    recv("IR", idt.at[yl], d_yl)
    relay("IF", idt.at[yl], d_yr)
    recv("B3O", G.at[x, 1 - z, c, :, L1], d_z)
    relay("C0", G.at[x, :, c], d_c)
    recv("A2R", G.at[xl, z, c, :, L0], d_xl)
    relay("A3R", G.at[xl, z, c, 0:32, L0], d_xr)
    recv("A2L", G.at[xr, z, c, :, L0], d_xr)
    relay("A3L", G.at[xr, z, c, 32:64, L0], d_xl)
    recv("B2R", G.at[xo, z, c, 0:32, L1], d_xl)
    recv("B2L", G.at[xo, z, c, 32:64, L1], d_xr)
    relay("B3F", G.at[xo, z, c, :, L1], d_z)
    recv("C0", G.at[x, :, 1 - c], d_c)
    back_step(x, True)
    up_step(x)
    recv("IL", idt.at[yr], d_yr)
    recv("IF", idt.at[yo], d_yl)
    onehot(0)
    recv("A2RZ", G.at[xl, 1 - z, c, :, L0], d_xl)
    relay("A3RZ", G.at[xl, 1 - z, c, 0:32, L0], d_xr)
    recv("A2LZ", G.at[xr, 1 - z, c, :, L0], d_xr)
    relay("A3LZ", G.at[xr, 1 - z, c, 32:64, L0], d_xl)
    recv("B3L", G.at[xl, 1 - z, c, :, L1], d_z)
    relay("CL", G.at[xl, :, c], d_c)
    recv("B3R", G.at[xr, 1 - z, c, :, L1], d_z)
    relay("CR", G.at[xr, :, c], d_c)
    recv("CL", G.at[xl, :, 1 - c], d_c)
    back_step(xl, False)
    up_step(xl)
    recv("CR", G.at[xr, :, 1 - c], d_c)
    back_step(xr, False)
    recv("A3R", G.at[xo, z, c, 0:32, L0], d_xl)
    recv("A3L", G.at[xo, z, c, 32:64, L0], d_xr)
    recv("A3RZ", G.at[xo, 1 - z, c, 0:32, L0], d_xl)
    recv("A3LZ", G.at[xo, 1 - z, c, 32:64, L0], d_xr)
    recv("B3F", G.at[xo, 1 - z, c, :, L1], d_z)
    relay("CF", G.at[xo, :, c], d_c)
    recv("JR", jdt.at[zl], d_zl)
    relay("JF", jdt.at[zl], d_zr)
    up_step(xr)
    recv("CF", G.at[xo, :, 1 - c], d_c)
    back_last(xo)

    down_term(0)
    y_send(0)
    y_send(1)
    down_term(1)
    y_send(2)
    down_term(2)
    up_step(xo)
    send("X1R", V.at[xo, :, 0:128], XR1, d_xr)
    send("X1L", V.at[xo, :, 128:256], XR2, d_xl)
    send("X2Rb", V.at[xr, :, 128:256], XFL.at[:, 128:256], d_xr)
    send("X2Lb", V.at[xl, :, 0:128], XFR.at[:, 0:128], d_xl)
    y_forward(0)
    y_send(3)
    down_term(3)
    y_forward(2)
    y_send(4)
    combine(0)
    z_rest(0)
    recv("X1R", XR1, d_xl)
    V[xr, :, 0:128] = (V[xr, :, 0:128].astype(F32) + XR1[...].astype(F32)).astype(BF)
    send("X2Ra", V.at[xr, :, 0:128], XFL.at[:, 0:128], d_xr)
    recv("X1L", XR2, d_xr)
    V[xl, :, 128:256] = (V[xl, :, 128:256].astype(F32) + XR2[...].astype(F32)).astype(BF)
    send("X2La", V.at[xl, :, 128:256], XFR.at[:, 128:256], d_xl)
    y_forward(3)
    y_send(5)
    y_forward(1)
    combine(2)
    z_rest(2)
    pass_on(0)
    y_forward(4)
    combine(3)
    z_rest(3)
    recv("JL", jdt.at[zr], d_zr)
    recv("JF", jdt.at[zo], d_zl)
    onehot(1)
    pass_on(2)
    recv("X2Rb", XFL.at[:, 128:256], d_xl)
    recv("X2Lb", XFR.at[:, 0:128], d_xr)
    recv("X2Ra", XFL.at[:, 0:128], d_xl)
    recv("X2La", XFR.at[:, 128:256], d_xr)
    for s in range(4):
        rows = slice(64 * s, 64 * s + 64)
        XS[s % 2, s // 2] = (V[x, :, rows].astype(F32) + XFL[:, rows].astype(F32) + XFR[:, rows].astype(F32)).astype(BF)
    send("Q2", XS.at[1 - c], QR.at[0:2], d_c)
    y_forward(5)
    combine(1)
    z_rest(1)
    recv("Q2", QR.at[0:2], d_c)
    XS[c, 1 - z] = (XS[c, 1 - z].astype(F32) + QR[1 - z].astype(F32)).astype(BF)
    send("Q1", XS.at[c, 1 - z], QR.at[2], d_z)
    combine(4)
    pass_on(3)
    z_rest(4)
    pass_on(1)
    combine(5)
    c_w.wait()
    input_grad(0)
    input_grad(1)
    recv("Q1", QR.at[2], d_z)

    def own_body(b, carry):
        total = XS[c, z, b].astype(F32) + QR[z, b].astype(F32) + QR[2, b].astype(F32)
        YB[y, b, 512:576, :] = (total * (scale_of(b) * norm)).astype(BF)
        return carry

    lax.fori_loop(0, 4, own_body, 0)
    y_send(6)
    pass_on(4)
    y_forward(6)
    finish(0)
    finish(1)
    finish(2)
    input_grad(2)
    combine(6)
    z_rest(5)
    pass_on(5)
    z_rest(6)
    finish(3)
    input_grad(3)
    pass_on(6)
    for k in (4, 5, 6):
        finish(k)
    gone(*list(sent))


def drain(ig, dg, ug, ig_h, dg_h, ug_h, sem):
    copies = [pltpu.make_async_copy(src, dst, sem.at[i]) for i, (src, dst) in enumerate(((ig, ig_h), (dg, dg_h), (ug, ug_h)))]
    for copy in copies:
        copy.start()
    for copy in copies:
        copy.wait()


def per_device(tokens, cotangent, value_weight, adapter_down, adapter_up, pair_ids, ranks):
    rows, width = tokens.shape
    norm = 1.0 / math.sqrt(rows * lax.axis_size("pair"))
    cot = cotangent.T
    up = jnp.swapaxes(adapter_up, 1, 2)
    any_spec = pl.BlockSpec(memory_space=pltpu.HBM)
    smem = pl.BlockSpec(memory_space=pltpu.SMEM)
    count = len(NAMES)
    vm = pltpu.VMEM
    import functools
    out = pl.pallas_call(
        functools.partial(kernel, norm),
        out_shape=(
            vm((2048, 512), BF),
            vm((3, 512, 128), BF),
            vm((3, 64, 128), BF),
        ),
        in_specs=[smem, smem] + [any_spec] * 5,
        out_specs=(pl.BlockSpec(memory_space=pltpu.VMEM),) * 3,
        scratch_shapes=[
            vm((4, 2, 2, 64, 2560), BF),
            vm((2048, 512), BF),
            vm((512, 1024), BF),
            vm((48, 512, 128), BF),
            vm((48, 64, 128), BF),
            vm((4, 512, 128), BF),
            vm((4, 512, 128), BF),
            vm((4, 128, 512), F32),
            vm((4, 128, 512), BF),
            vm((4, 4, 576, 128), BF),
            vm((4, 3, 576, 128), BF),
            vm((3, 288, 128), BF),
            vm((3, 288, 128), BF),
            vm((3, 576, 128), BF),
            vm((3, 576, 128), BF),
            vm((4, 4, 256, 128), BF),
            vm((4, 128, 128), BF),
            vm((4, 128, 128), BF),
            vm((4, 256, 128), BF),
            vm((4, 256, 128), BF),
            vm((2, 2, 4, 64, 128), BF),
            vm((3, 4, 64, 128), BF),
            vm((4, 8, 256), jnp.int32),
            vm((4, 8, 256), jnp.int32),
            vm((2, 192, 256), BF),
            pltpu.SemaphoreType.DMA((count,)),
            pltpu.SemaphoreType.DMA((count,)),
            pltpu.SemaphoreType.DMA((5,)),
        ],
        compiler_params=pltpu.CompilerParams(
            collective_id=0, has_side_effects=True, vmem_limit_bytes=60 * 1024 * 1024
        ),
    )(pair_ids, ranks, tokens, cot, value_weight, adapter_down, up)
    out = [pltpu.with_memory_space_constraint(part, pltpu.VMEM) for part in out]
    out = pl.pallas_call(
        drain,
        out_shape=tuple(jax.ShapeDtypeStruct(part.shape, BF) for part in out),
        in_specs=[pl.BlockSpec(memory_space=pltpu.VMEM)] * 3,
        out_specs=(any_spec,) * 3,
        scratch_shapes=[pltpu.SemaphoreType.DMA((3,))],
        compiler_params=pltpu.CompilerParams(vmem_limit_bytes=1024 * 1024),
    )(*out)
    return out[0], out[1], jnp.swapaxes(out[2], 1, 2)


def solution(mesh):
    placed = (
        P("pair", "fsdp"),
        P("pair", "fsdp"),
        P("fsdp", None),
        P(None, "fsdp", None),
        P(None, None, "fsdp"),
        P("pair"),
        P(),
    )
    return jax.shard_map(
        per_device,
        mesh=mesh,
        in_specs=placed,
        out_specs=(P("pair", "fsdp"), P("pair", "fsdp", None), P("pair", None, "fsdp")),
        check_vma=False,
    )
```

time: 97.2 us -> 75.1 us (0.77); the launches traced: 97.1 us -> 73.7 us
  Pallas kernels: 92 us -> 73 us
  local copies, waits for them, and re-layouts: 4.47 us -> 0 us
    pallas_call x1 -> x2, Pallas kernels: 92 us -> 73 us  [the longest x1 71.6 us: per_device(): pl.pallas_call(functools.partial(kernel, norm), out_shape=(vm((2048, 512)...]
    unnamed x7 -> x0, local copies, waits for them, and re-layouts: 4.47 us -> none
where the time goes in v2:
time: 75.1 us; the launch traced here: 73.7 us
  Pallas kernels  73 us (97%)
    pallas_call x1, Pallas kernels, per_device(): pl.pallas_call(functools.partial(kernel, norm), out_shape=(vm((2048, 512)...  71.6 us

profile of v2, /device:TPU:1, one launch (start us, length us, event | category | flops | bytes accessed | tf_op | source)
XLA Modules:
  0.0 73.7 jit_solution(12699059725648122755)
XLA Ops:
  0.6 71.6 %shard_map.94 = (bf16[2048,512]{1,0:T(8,128)(2,1)S(1)}, bf16[3,512,128]{2,1,0:T(8,128)(2,1)S(1)}, bf16[3,64,128]{2,1,0:T(8,128)(2,1)S(1)}) custom-call(s32[4]{0:T(128)} %ids.1, s32[48]{0:T(128)} %ranks.1, bf16[2048,512]{1,0:T(8,128)(2,1)} %tok_h.1, bf16[64,2048]{1,0:T(8,128)(2,1)} %bitcast.4, bf16[512,1024]{1,0:T(8,128)(2,1)} %w_h.1, ...), custom_call_target="tpu_custom_call" | custom-call | tf_op jit(solution)/shard_map/pallas_call | solution.py:430
  72.2 1.5 %shard_map.95 = (bf16[2048,512]{1,0:T(8,128)(2,1)}, bf16[3,512,128]{2,1,0:T(8,128)(2,1)}, bf16[3,64,128]{2,1,0:T(8,128)(2,1)}) custom-call(bf16[2048,512]{1,0:T(8,128)(2,1)S(1)} %get-tuple-element.9.ig, bf16[3,512,128]{2,1,0:T(8,128)(2,1)S(1)} %get-tuple-element.10.dg, bf16[3,64,128]{2,1,0:T(8,128)(2,1)S(1)} %get-tuple-element.11.ug), custom_call_target="tpu_custom_call" | custom-call | tf_op jit(solution)/shard_map/pallas_call | solution.py:474

commit v3 on v2

--- a/solution.py
+++ b/solution.py
@@ -11,10 +11,10 @@
 BF = jnp.bfloat16
 F32 = jnp.float32
 
-NAMES = ["A1", "B1R", "B1L", "B3O", "A2R", "A2L", "A2RZ", "A2LZ", "B2R", "B2L", "B3L", "B3R", "A3R", "A3L", "A3RZ", "A3LZ", "B3F", "C0", "CL", "CR", "CF"]
+NAMES = ["A1", "B1R", "B1L", "B3O", "A2R", "A2L", "A2RZ", "A2LZ", "B2R", "B2L", "B3L", "B3R", "A3R", "A3L", "A3RZ", "A3LZ", "B3F", "C0", "CL", "CR", "CE", "CF"]
 NAMES += ["IR", "IL", "IF", "JR", "JL", "JF"]
 NAMES += ["X1R", "X1L", "X2Rb", "X2Lb", "X2Ra", "X2La", "Q1", "Q2"]
-CHUNKS = [(0, 32), (32, 96), (128, 64), (192, 96), (288, 128), (416, 96), (512, 64)]
+CHUNKS = [(0, 32), (32, 160), (192, 64), (256, 96), (352, 96), (448, 64), (512, 64)]
 SWAPPED = 1
 for _k in range(len(CHUNKS)):
     NAMES += [n + str(_k) for n in ("YR", "YL", "YFR", "YFL", "Z1R", "Z1L", "Z2Rb", "Z2Lb", "Z2Ra", "Z2La")]
@@ -25,9 +25,9 @@
     return lax.dot_general(a, b, (((ca,), (cb,)), ((), ())), preferred_element_type=F32)
 
 
-def kernel(norm, ids, ranks, tok_h, cot_h, w_h, a_h, b_h, igv, dgv, ugv,
+def kernel(norm, ids_h, ranks_h, tok_h, cot_h, w_h, a_h, b_h, igv, dgv, ugv,
            G, xv, wv, av, bv, asel, low, backf, backb, YB, ZB, R1, R2, FL, FR,
-           V, XR1, XR2, XFL, XFR, XS, QR, idt, jdt, Lm, ss, rs, ls):
+           V, XR1, XR2, XFL, XFR, XS, QR, idt, jdt, Lm, ids, ranks, ss, rs, ls):
     f = lax.axis_index("fsdp")
     q = lax.axis_index("pair")
     x, z, c = f // 4, (f // 2) % 2, f % 2
@@ -70,19 +70,16 @@
                                      device_id=device, device_id_type=MESH).wait_recv()
 
     c_cot = pltpu.make_async_copy(cot_h, G.at[x, z, c, :, 0:2048], ls.at[0])
-    c_cot.start()
+    c_ids = pltpu.make_async_copy(ids_h, ids, ls.at[5])
     c_b = pltpu.make_async_copy(b_h, bv, ls.at[1])
-    c_b.start()
+    c_ranks = pltpu.make_async_copy(ranks_h, ranks, ls.at[6])
+    for copy in (c_cot, c_ids, c_b, c_ranks):
+        copy.start()
 
     barrier = pltpu.get_barrier_semaphore()
     for device in (d_z, d_c, d_xr, d_xl, d_yr, d_yl, d_zr, d_zl):
         pl.semaphore_signal(barrier, inc=1, device_id=device, device_id_type=MESH)
 
-    lane = lax.broadcasted_iota(jnp.int32, (8, 256), 1)
-    part = (lane >> 4) & 3
-    tile = jnp.where(part == 0, ids[0], jnp.where(part == 1, ids[1], jnp.where(part == 2, ids[2], ids[3])))
-    idt[y] = tile
-    jdt[zh] = tile
     c_x = pltpu.make_async_copy(tok_h, xv, ls.at[2])
     c_a = pltpu.make_async_copy(a_h, av, ls.at[3])
     c_w = pltpu.make_async_copy(w_h, wv, ls.at[4])
@@ -96,6 +93,8 @@
     pl.semaphore_wait(barrier, 8)
     relay("A1", G.at[x, z, c, :, L0], d_z)
     c_b.wait()
+    c_ids.wait()
+    c_ranks.wait()
     for b in range(4):
         G[x, z, c, :, 2048 + 128 * b:2176 + 128 * b] = bv[ids[b]]
     relay("B1R", G.at[x, z, c, :, L1], d_xr)
@@ -105,6 +104,11 @@
     relay("A2L", G.at[x, z, c, :, L0], d_xl)
     for copy in (c_x, c_a, c_w):
         copy.start()
+    lane = lax.broadcasted_iota(jnp.int32, (8, 256), 1)
+    part = (lane >> 4) & 3
+    tile = jnp.where(part == 0, ids[0], jnp.where(part == 1, ids[1], jnp.where(part == 2, ids[2], ids[3])))
+    idt[y] = tile
+    jdt[zh] = tile
     relay("IR", idt.at[y], d_yr)
     relay("IL", idt.at[y], d_yl)
     relay("JR", jdt.at[zh], d_zr)
@@ -248,11 +252,10 @@
         for b in range(4):
             value = dot(backb[b], xv[512 * b:512 * b + 512, 128 * k:128 * k + 128])
             value = (value.T * (scale_of(b) * norm)).astype(BF)
-            if k == 0:
-                YB[y, b, 0:32, :] = value[0:32]
-                YB[zh, b, 32:128, :] = value[32:128]
-            else:
-                YB[y, b, 128 * k:128 * k + 128, :] = value
+            for i, (r0, n) in enumerate(CHUNKS):
+                lo, hi = max(r0, 128 * k), min(r0 + n, 128 * k + 128)
+                if lo < hi:
+                    YB[role[i][0][0], b, lo:hi, :] = value[lo - 128 * k:hi - 128 * k]
 
     def input_grad(b):
         ad = scale_of(b)[:, 0:1]
@@ -268,6 +271,56 @@
             return carry
 
         lax.fori_loop(0, 4, body, 0)
+
+    me, other = c, 1 - c
+
+    def up_exchange():
+        up_step(xo)
+        send("X1R", V.at[xo, :, 0:128], XR1, d_xr)
+        send("X1L", V.at[xo, :, 128:256], XR2, d_xl)
+
+    def up_direct():
+        send("X2Rb", V.at[xr, :, 128:256], XFL.at[:, 128:256], d_xr)
+        send("X2Lb", V.at[xl, :, 0:128], XFR.at[:, 0:128], d_xl)
+
+    def up_pass():
+        recv("X1R", XR1, d_xl)
+        V[xr, :, 0:128] = (V[xr, :, 0:128].astype(F32) + XR1[...].astype(F32)).astype(BF)
+        send("X2Ra", V.at[xr, :, 0:128], XFL.at[:, 0:128], d_xr)
+        recv("X1L", XR2, d_xr)
+        V[xl, :, 128:256] = (V[xl, :, 128:256].astype(F32) + XR2[...].astype(F32)).astype(BF)
+        send("X2La", V.at[xl, :, 128:256], XFR.at[:, 128:256], d_xl)
+
+    def up_split():
+        recv("X2Rb", XFL.at[:, 128:256], d_xl)
+        recv("X2Lb", XFR.at[:, 0:128], d_xr)
+        recv("X2Ra", XFL.at[:, 0:128], d_xl)
+        recv("X2La", XFR.at[:, 128:256], d_xr)
+        for s in range(4):
+            rows = slice(64 * s, 64 * s + 64)
+            total = V[x, :, rows].astype(F32) + XFL[:, rows].astype(F32) + XFR[:, rows].astype(F32)
+            XS[s % 2, s // 2] = total.astype(BF)
+        send("Q2", XS.at[other], QR.at[0:2], d_c)
+
+    def up_cross():
+        recv("Q2", QR.at[0:2], d_c)
+        XS[me, 1 - z] = (XS[me, 1 - z].astype(F32) + QR[1 - z].astype(F32)).astype(BF)
+        send("Q1", XS.at[me, 1 - z], QR.at[2], d_z)
+
+    def up_own():
+        recv("Q1", QR.at[2], d_z)
+
+        def body(b, carry):
+            total = XS[me, z, b].astype(F32) + QR[z, b].astype(F32) + QR[2, b].astype(F32)
+            YB[y, b, 512:576, :] = (total * (scale_of(b) * norm)).astype(BF)
+            return carry
+
+        lax.fori_loop(0, 4, body, 0)
+
+    def column_onehot():
+        recv("JL", jdt.at[zr], d_zr)
+        recv("JF", jdt.at[zo], d_zl)
+        onehot(1)
 
     c_a.wait()
     c_x.wait()
@@ -306,106 +359,83 @@
     relay("CL", G.at[xl, :, c], d_c)
     recv("B3R", G.at[xr, 1 - z, c, :, L1], d_z)
     relay("CR", G.at[xr, :, c], d_c)
+    recv("A3R", G.at[xo, z, c, 0:32, L0], d_xl)
+    recv("A3L", G.at[xo, z, c, 32:64, L0], d_xr)
+    relay("CE", G.at[xo, z, c], d_c)
+    recv("JR", jdt.at[zl], d_zl)
+    relay("JF", jdt.at[zl], d_zr)
     recv("CL", G.at[xl, :, 1 - c], d_c)
     back_step(xl, False)
-    up_step(xl)
-    recv("CR", G.at[xr, :, 1 - c], d_c)
-    back_step(xr, False)
-    recv("A3R", G.at[xo, z, c, 0:32, L0], d_xl)
-    recv("A3L", G.at[xo, z, c, 32:64, L0], d_xr)
     recv("A3RZ", G.at[xo, 1 - z, c, 0:32, L0], d_xl)
     recv("A3LZ", G.at[xo, 1 - z, c, 32:64, L0], d_xr)
     recv("B3F", G.at[xo, 1 - z, c, :, L1], d_z)
-    relay("CF", G.at[xo, :, c], d_c)
-    recv("JR", jdt.at[zl], d_zl)
-    relay("JF", jdt.at[zl], d_zr)
-    up_step(xr)
-    recv("CF", G.at[xo, :, 1 - c], d_c)
+    relay("CF", G.at[xo, 1 - z, c], d_c)
+    recv("CR", G.at[xr, :, 1 - c], d_c)
+    back_step(xr, False)
+    recv("CE", G.at[xo, z, 1 - c], d_c)
+    recv("CF", G.at[xo, 1 - z, 1 - c], d_c)
     back_last(xo)
 
     down_term(0)
     y_send(0)
-    y_send(1)
     down_term(1)
     y_send(2)
+    y_send(1)
+    up_exchange()
     down_term(2)
-    up_step(xo)
-    send("X1R", V.at[xo, :, 0:128], XR1, d_xr)
-    send("X1L", V.at[xo, :, 128:256], XR2, d_xl)
-    send("X2Rb", V.at[xr, :, 128:256], XFL.at[:, 128:256], d_xr)
-    send("X2Lb", V.at[xl, :, 0:128], XFR.at[:, 0:128], d_xl)
-    y_forward(0)
     y_send(3)
     down_term(3)
+    up_step(xr)
+    up_step(xl)
+    up_direct()
+    y_forward(0)
     y_forward(2)
+    y_send(5)
+    up_pass()
     y_send(4)
     combine(0)
+    column_onehot()
     z_rest(0)
-    recv("X1R", XR1, d_xl)
-    V[xr, :, 0:128] = (V[xr, :, 0:128].astype(F32) + XR1[...].astype(F32)).astype(BF)
-    send("X2Ra", V.at[xr, :, 0:128], XFL.at[:, 0:128], d_xr)
-    recv("X1L", XR2, d_xr)
-    V[xl, :, 128:256] = (V[xl, :, 128:256].astype(F32) + XR2[...].astype(F32)).astype(BF)
-    send("X2La", V.at[xl, :, 128:256], XFR.at[:, 128:256], d_xl)
-    y_forward(3)
-    y_send(5)
-    y_forward(1)
     combine(2)
     z_rest(2)
-    pass_on(0)
-    y_forward(4)
-    combine(3)
-    z_rest(3)
-    recv("JL", jdt.at[zr], d_zr)
-    recv("JF", jdt.at[zo], d_zl)
-    onehot(1)
-    pass_on(2)
-    recv("X2Rb", XFL.at[:, 128:256], d_xl)
-    recv("X2Lb", XFR.at[:, 0:128], d_xr)
-    recv("X2Ra", XFL.at[:, 0:128], d_xl)
-    recv("X2La", XFR.at[:, 128:256], d_xr)
-    for s in range(4):
-        rows = slice(64 * s, 64 * s + 64)
-        XS[s % 2, s // 2] = (V[x, :, rows].astype(F32) + XFL[:, rows].astype(F32) + XFR[:, rows].astype(F32)).astype(BF)
-    send("Q2", XS.at[1 - c], QR.at[0:2], d_c)
-    y_forward(5)
-    combine(1)
-    z_rest(1)
-    recv("Q2", QR.at[0:2], d_c)
-    XS[c, 1 - z] = (XS[c, 1 - z].astype(F32) + QR[1 - z].astype(F32)).astype(BF)
-    send("Q1", XS.at[c, 1 - z], QR.at[2], d_z)
-    combine(4)
-    pass_on(3)
-    z_rest(4)
-    pass_on(1)
-    combine(5)
+    y_forward(3)
     c_w.wait()
     input_grad(0)
+    y_forward(5)
+    y_forward(1)
+    up_split()
+    y_forward(4)
     input_grad(1)
-    recv("Q1", QR.at[2], d_z)
-
-    def own_body(b, carry):
-        total = XS[c, z, b].astype(F32) + QR[z, b].astype(F32) + QR[2, b].astype(F32)
-        YB[y, b, 512:576, :] = (total * (scale_of(b) * norm)).astype(BF)
-        return carry
-
-    lax.fori_loop(0, 4, own_body, 0)
+    up_cross()
+    combine(3)
+    combine(4)
+    z_rest(4)
+    input_grad(2)
+    z_rest(3)
+    up_own()
     y_send(6)
+    combine(1)
+    pass_on(3)
+    combine(5)
+    z_rest(5)
+    y_forward(6)
+    z_rest(1)
     pass_on(4)
-    y_forward(6)
+    combine(6)
+    pass_on(1)
+    pass_on(2)
+    pass_on(0)
+    input_grad(3)
+    pass_on(5)
+    finish(3)
+    z_rest(6)
+    finish(1)
+    pass_on(6)
+    finish(2)
+    finish(5)
     finish(0)
-    finish(1)
-    finish(2)
-    input_grad(2)
-    combine(6)
-    z_rest(5)
-    pass_on(5)
-    z_rest(6)
-    finish(3)
-    input_grad(3)
-    pass_on(6)
-    for k in (4, 5, 6):
-        finish(k)
+    finish(4)
+    finish(6)
     gone(*list(sent))
 
 
@@ -423,7 +453,6 @@
     cot = cotangent.T
     up = jnp.swapaxes(adapter_up, 1, 2)
     any_spec = pl.BlockSpec(memory_space=pltpu.HBM)
-    smem = pl.BlockSpec(memory_space=pltpu.SMEM)
     count = len(NAMES)
     vm = pltpu.VMEM
     import functools
@@ -434,7 +463,7 @@
             vm((3, 512, 128), BF),
             vm((3, 64, 128), BF),
         ),
-        in_specs=[smem, smem] + [any_spec] * 5,
+        in_specs=[any_spec] * 7,
         out_specs=(pl.BlockSpec(memory_space=pltpu.VMEM),) * 3,
         scratch_shapes=[
             vm((4, 2, 2, 64, 2560), BF),
@@ -462,9 +491,11 @@
             vm((4, 8, 256), jnp.int32),
             vm((4, 8, 256), jnp.int32),
             vm((2, 192, 256), BF),
+            pltpu.SMEM((4,), jnp.int32),
+            pltpu.SMEM((48,), jnp.int32),
             pltpu.SemaphoreType.DMA((count,)),
             pltpu.SemaphoreType.DMA((count,)),
-            pltpu.SemaphoreType.DMA((5,)),
+            pltpu.SemaphoreType.DMA((7,)),
         ],
         compiler_params=pltpu.CompilerParams(
             collective_id=0, has_side_effects=True, vmem_limit_bytes=60 * 1024 * 1024

time: 75.1 us -> 70.9 us (0.944)
  Pallas kernels: 73 us -> 69.4 us
    pallas_call x1, Pallas kernels: 71.6 us -> 67.9 us  [per_device(): pl.pallas_call(functools.partial(kernel, norm), out_shape=(vm((2048, 512)...]
where the time goes in v3:
time: 70.9 us; the launch traced here: 70 us
  Pallas kernels  69.4 us (98%)
    pallas_call x1, Pallas kernels, per_device(): pl.pallas_call(functools.partial(kernel, norm), out_shape=(vm((2048, 512)...  67.9 us
    pallas_call x1, Pallas kernels, per_device(): pl.pallas_call(drain, out_shape=tuple((jax.ShapeDtypeStruct(part.shape, B...  1.47 us

profile of v3, /device:TPU:1, one launch (start us, length us, event | category | flops | bytes accessed | tf_op | source)
XLA Modules:
  0.0 70.0 jit_solution(2675427986916316069)
XLA Ops:
  0.6 67.9 %shard_map.94 = (bf16[2048,512]{1,0:T(8,128)(2,1)S(1)}, bf16[3,512,128]{2,1,0:T(8,128)(2,1)S(1)}, bf16[3,64,128]{2,1,0:T(8,128)(2,1)S(1)}) custom-call(s32[4]{0:T(128)} %ids_h.1, s32[48]{0:T(128)} %ranks_h.1, bf16[2048,512]{1,0:T(8,128)(2,1)} %tok_h.1, bf16[64,2048]{1,0:T(8,128)(2,1)} %bitcast.4, bf16[512,1024]{1,0:T(8,128)(2,1)} %w_h.1, ...), custom_call_target="tpu_custom_call" | custom-call | tf_op jit(solution)/shard_map/pallas_call | solution.py:459
  68.6 1.5 %shard_map.95 = (bf16[2048,512]{1,0:T(8,128)(2,1)}, bf16[3,512,128]{2,1,0:T(8,128)(2,1)}, bf16[3,64,128]{2,1,0:T(8,128)(2,1)}) custom-call(bf16[2048,512]{1,0:T(8,128)(2,1)S(1)} %get-tuple-element.9.ig, bf16[3,512,128]{2,1,0:T(8,128)(2,1)S(1)} %get-tuple-element.10.dg, bf16[3,64,128]{2,1,0:T(8,128)(2,1)S(1)} %get-tuple-element.11.ug), custom_call_target="tpu_custom_call" | custom-call | tf_op jit(solution)/shard_map/pallas_call | solution.py:505

commit v4 on v3

--- a/solution.py
+++ b/solution.py
@@ -14,7 +14,7 @@
 NAMES = ["A1", "B1R", "B1L", "B3O", "A2R", "A2L", "A2RZ", "A2LZ", "B2R", "B2L", "B3L", "B3R", "A3R", "A3L", "A3RZ", "A3LZ", "B3F", "C0", "CL", "CR", "CE", "CF"]
 NAMES += ["IR", "IL", "IF", "JR", "JL", "JF"]
 NAMES += ["X1R", "X1L", "X2Rb", "X2Lb", "X2Ra", "X2La", "Q1", "Q2"]
-CHUNKS = [(0, 32), (32, 160), (192, 64), (256, 96), (352, 96), (448, 64), (512, 64)]
+CHUNKS = [(0, 32), (32, 160), (192, 64), (256, 64), (320, 96), (416, 96), (512, 64)]
 SWAPPED = 1
 for _k in range(len(CHUNKS)):
     NAMES += [n + str(_k) for n in ("YR", "YL", "YFR", "YFL", "Z1R", "Z1L", "Z2Rb", "Z2Lb", "Z2Ra", "Z2La")]
@@ -84,7 +84,7 @@
     c_a = pltpu.make_async_copy(a_h, av, ls.at[3])
     c_w = pltpu.make_async_copy(w_h, wv, ls.at[4])
 
-    L0, L1 = slice(0, 1408), slice(1408, 2560)
+    L0, L1 = slice(0, 1280), slice(1280, 2560)
 
     def relay(name, part, device):
         send(name, part, part, device)

time: 70.9 us -> 71.9 us (1.014); the launches traced: 70 us -> 71.8 us
  Pallas kernels: 69.4 us -> 71.1 us
    pallas_call x1, Pallas kernels: 67.9 us -> 69.7 us  [per_device(): pl.pallas_call(functools.partial(kernel, norm), out_shape=(vm((2048, 512)...]
where the time goes in v4:
time: 71.9 us; the launch traced here: 71.8 us
  Pallas kernels  71.1 us (99%)
    pallas_call x1, Pallas kernels, per_device(): pl.pallas_call(functools.partial(kernel, norm), out_shape=(vm((2048, 512)...  69.7 us
    pallas_call x1, Pallas kernels, per_device(): pl.pallas_call(drain, out_shape=tuple((jax.ShapeDtypeStruct(part.shape, B...  1.47 us

profile of v4, /device:TPU:1, one launch (start us, length us, event | category | flops | bytes accessed | tf_op | source)
XLA Modules:
  0.0 71.8 jit_solution(14652727146787633690)
XLA Ops:
  0.6 69.7 %shard_map.94 = (bf16[2048,512]{1,0:T(8,128)(2,1)S(1)}, bf16[3,512,128]{2,1,0:T(8,128)(2,1)S(1)}, bf16[3,64,128]{2,1,0:T(8,128)(2,1)S(1)}) custom-call(s32[4]{0:T(128)} %ids_h.1, s32[48]{0:T(128)} %ranks_h.1, bf16[2048,512]{1,0:T(8,128)(2,1)} %tok_h.1, bf16[64,2048]{1,0:T(8,128)(2,1)} %bitcast.4, bf16[512,1024]{1,0:T(8,128)(2,1)} %w_h.1, ...), custom_call_target="tpu_custom_call" | custom-call | tf_op jit(solution)/shard_map/pallas_call | solution.py:459
  70.3 1.5 %shard_map.95 = (bf16[2048,512]{1,0:T(8,128)(2,1)}, bf16[3,512,128]{2,1,0:T(8,128)(2,1)}, bf16[3,64,128]{2,1,0:T(8,128)(2,1)}) custom-call(bf16[2048,512]{1,0:T(8,128)(2,1)S(1)} %get-tuple-element.9.ig, bf16[3,512,128]{2,1,0:T(8,128)(2,1)S(1)} %get-tuple-element.10.dg, bf16[3,64,128]{2,1,0:T(8,128)(2,1)S(1)} %get-tuple-element.11.ug), custom_call_target="tpu_custom_call" | custom-call | tf_op jit(solution)/shard_map/pallas_call | solution.py:505

commit v5 on v4

--- a/solution.py
+++ b/solution.py
@@ -14,7 +14,7 @@
 NAMES = ["A1", "B1R", "B1L", "B3O", "A2R", "A2L", "A2RZ", "A2LZ", "B2R", "B2L", "B3L", "B3R", "A3R", "A3L", "A3RZ", "A3LZ", "B3F", "C0", "CL", "CR", "CE", "CF"]
 NAMES += ["IR", "IL", "IF", "JR", "JL", "JF"]
 NAMES += ["X1R", "X1L", "X2Rb", "X2Lb", "X2Ra", "X2La", "Q1", "Q2"]
-CHUNKS = [(0, 32), (32, 160), (192, 64), (256, 64), (320, 96), (416, 96), (512, 64)]
+CHUNKS = [(0, 32), (32, 160), (192, 64), (256, 96), (352, 96), (448, 64), (512, 64)]
 SWAPPED = 1
 for _k in range(len(CHUNKS)):
     NAMES += [n + str(_k) for n in ("YR", "YL", "YFR", "YFL", "Z1R", "Z1L", "Z2Rb", "Z2Lb", "Z2Ra", "Z2La")]

time: 71.9 us -> 70.8 us (0.985)
  Pallas kernels: 71.1 us -> 69.8 us
    pallas_call x1, Pallas kernels: 69.7 us -> 68.3 us  [per_device(): pl.pallas_call(functools.partial(kernel, norm), out_shape=(vm((2048, 512)...]
where the time goes in v5:
time: 70.8 us; the launch traced here: 70.4 us
  Pallas kernels  69.8 us (99%)
    pallas_call x1, Pallas kernels, per_device(): pl.pallas_call(functools.partial(kernel, norm), out_shape=(vm((2048, 512)...  68.3 us
    pallas_call x1, Pallas kernels, per_device(): pl.pallas_call(drain, out_shape=tuple((jax.ShapeDtypeStruct(part.shape, B...  1.47 us

profile of v5, /device:TPU:1, one launch (start us, length us, event | category | flops | bytes accessed | tf_op | source)
XLA Modules:
  0.0 70.4 jit_solution(7071195680508064473)
XLA Ops:
  0.6 68.3 %shard_map.94 = (bf16[2048,512]{1,0:T(8,128)(2,1)S(1)}, bf16[3,512,128]{2,1,0:T(8,128)(2,1)S(1)}, bf16[3,64,128]{2,1,0:T(8,128)(2,1)S(1)}) custom-call(s32[4]{0:T(128)} %ids_h.1, s32[48]{0:T(128)} %ranks_h.1, bf16[2048,512]{1,0:T(8,128)(2,1)} %tok_h.1, bf16[64,2048]{1,0:T(8,128)(2,1)} %bitcast.4, bf16[512,1024]{1,0:T(8,128)(2,1)} %w_h.1, ...), custom_call_target="tpu_custom_call" | custom-call | tf_op jit(solution)/shard_map/pallas_call | solution.py:459
  69.0 1.5 %shard_map.95 = (bf16[2048,512]{1,0:T(8,128)(2,1)}, bf16[3,512,128]{2,1,0:T(8,128)(2,1)}, bf16[3,64,128]{2,1,0:T(8,128)(2,1)}) custom-call(bf16[2048,512]{1,0:T(8,128)(2,1)S(1)} %get-tuple-element.9.ig, bf16[3,512,128]{2,1,0:T(8,128)(2,1)S(1)} %get-tuple-element.10.dg, bf16[3,64,128]{2,1,0:T(8,128)(2,1)S(1)} %get-tuple-element.11.ug), custom_call_target="tpu_custom_call" | custom-call | tf_op jit(solution)/shard_map/pallas_call | solution.py:505
